TPU v7x, 32 devices: a whole 2x2x4 slice. The times are simulated.
32 devices in a mesh: group: 2 (over x), context: 16 (over z, y, core).
Axes of the slice: x: 2, y: 2, z: 4, core: 2. Of those that a mesh axis runs over, the one named last changes fastest.
Arguments:
- features: bfloat16 [4096, 3, 8192], P(('group', 'context')), parts along dimension 0, may hold values from -6 to 6
- base_rows: bfloat16 [4, 3, 8192], replicated, may hold values from -6 to 6
- positions: int32 [128], P('group'), parts along dimension 0, may hold values from 0 to 2047, as said below
- alt_bases: int32 [128], P('group'), parts along dimension 0, may hold values from 0 to 3
- decay_rate: float32 [16, 8192], replicated, may hold values from 9.765625e-06 to 0.03
- residue: float32 [16, 8192], replicated, may hold values from -5 to 5
- skip_gain: float32 [8192], replicated, may hold values from 0.5 to 1.5
Outputs:
- ref_out: bfloat16 [4096, 8192], P(('group', 'context')), parts along dimension 0
- effect: bfloat16 [4096, 8192], P(('group', 'context')), parts along dimension 0
- channel_score: float32 [16384], P(('group', 'context')), parts along dimension 0
There are 2 independent parts, one for each index of `group`. A program takes and returns all parts, laid end to end along the dimension named above; an argument that names none is the same for every part. Nothing has to cross between parts.
Inputs may be any that keep to these rules, and one draw needn't show every extreme that they name: `positions`: ascending; exactly one lies in each aligned stretch of 32 positions; the first is 0 and the last is 2047. `alt_bases`: an index into the first dimension of base_rows.
All inputs are finite; a program needn't handle non-finite values.
Results may differ from a plain program's by a relative error of at most 0.0005.
Values may be sent and summed in bfloat16 or wider, within the bound.
A program may use at most 384 MiB of HBM per device.

v0:
```python
import functools

import jax
import jax.numpy as jnp
import numpy as np
from jax import lax
from jax.experimental import pallas as pl
from jax.experimental.pallas import tpu as pltpu
from jax.sharding import PartitionSpec as P

F32 = jnp.float32
BF16 = jnp.bfloat16
MESH = pl.DeviceIdType.MESH
RATE_MAX = 0.03
KD = 10
KB = 7


def cheb_table(length):
    nodes = 64
    theta = (np.arange(nodes) + 0.5) * np.pi / nodes
    rate = (np.cos(theta) + 1.0) * (RATE_MAX / 2)
    values = np.exp(-rate[None] * np.arange(length)[:, None])
    basis = np.cos(np.arange(16)[:, None] * theta[None])
    table = 2.0 / nodes * values @ basis.T
    table[:, 0] *= 0.5
    return table


def split3_lhs(a):
    a = a.astype(np.float32)
    hi = a.astype(jnp.bfloat16)
    lo = (a - hi.astype(np.float32)).astype(jnp.bfloat16)
    return np.concatenate([hi, lo, hi], axis=1)


def split3_rhs(x):
    hi = x.astype(BF16)
    lo = (x - hi.astype(F32)).astype(BF16)
    return jnp.concatenate([hi, hi, lo], axis=0)


def pad_rows(a, rows):
    return np.concatenate([a, np.zeros((rows - a.shape[0],) + a.shape[1:])], axis=0)


def pad_cols(a, cols):
    return np.concatenate([a, np.zeros((a.shape[0], cols - a.shape[1]))], axis=1)


def cheb_terms(rate, count):
    x = rate * (2.0 / RATE_MAX) - 1.0
    terms = [jnp.ones_like(x), x]
    while len(terms) < count:
        terms.append(2.0 * x * terms[-1] - terms[-2])
    return terms


def modal_coef(rate, residue):
    z = 2.0 * rate
    tail = 1.0 - z * (1.0 / 2) * (1.0 - z * (1.0 / 3) * (1.0 - z * (1.0 / 4) * (1.0 - z * (1.0 / 5) * (1.0 - z * (1.0 / 6)))))
    return residue * jnp.sqrt(z * tail)


def combine(nv, length, lags, in_ref, my_rate, my_residue, out_ref):
    devices = in_ref.shape[0]
    height = KD + nv
    row = lax.broadcasted_iota(jnp.int32, (devices, 128), 0)

    def before(ends, rate_n):
        ends = jnp.where(row >= 1, pltpu.roll(ends, 1, 0), 0.0)
        hop = 1
        while hop < devices:
            fade = jnp.exp(rate_n * (-float(length) * hop))
            ends = ends + fade * jnp.where(row >= hop, pltpu.roll(ends, hop, 0), 0.0)
            hop *= 2
        return ends

    for c in range(my_rate.shape[1] // 128):
        rate = my_rate[:, c * 128 : (c + 1) * 128]
        terms = cheb_terms(rate, KD)
        lead = modal_coef(rate, my_residue[:, c * 128 : (c + 1) * 128]) * jnp.exp(-rate)
        leads = [lead * term for term in terms]
        moments = [in_ref[:, c * height + k, :] for k in range(KD)]
        subs = [in_ref[:, c * height + KD + i, :] for i in range(nv)]
        base = [jnp.zeros((devices, 128), F32) for _ in range(KD)]
        change = [jnp.zeros((devices, 128), F32) for _ in range(KD)]
        for n in range(rate.shape[0]):
            rate_n = rate[n : n + 1]
            ends = terms[0][n : n + 1] * moments[0]
            for k in range(1, KD):
                ends = ends + terms[k][n : n + 1] * moments[k]
            shifted = jnp.exp(-rate_n * lags[0]) * subs[0]
            for i in range(1, nv):
                shifted = shifted + jnp.exp(-rate_n * lags[i]) * subs[i]
            ends, shifted = before(ends, rate_n), before(shifted, rate_n)
            for k in range(KD):
                base[k] = base[k] + leads[k][n : n + 1] * ends
                change[k] = change[k] + leads[k][n : n + 1] * shifted
        for k in range(KD):
            out_ref[:, c * 2 * KD + k, :] = base[k]
            out_ref[:, c * 2 * KD + KD + k, :] = change[k]


def greet(devices):
    me = lax.axis_index("context")
    barrier = pltpu.get_barrier_semaphore()
    for hop in range(1, devices):
        pl.semaphore_signal(
            barrier, inc=1, device_id={"context": lax.rem(me + hop, devices)}, device_id_type=MESH
        )
    return lambda: pl.semaphore_wait(barrier, devices - 1)


def hand_out(src_ref, dst_ref, own_sem, send_sems, recv_sems):
    devices = src_ref.shape[0]
    me = lax.axis_index("context")
    copies = []
    for hop in range(1, devices):
        peer = lax.rem(me + hop, devices)
        copies.append(
            pltpu.make_async_remote_copy(
                src_ref=src_ref.at[peer],
                dst_ref=dst_ref.at[me],
                send_sem=send_sems.at[hop],
                recv_sem=recv_sems.at[hop],
                device_id={"context": peer},
                device_id_type=MESH,
            )
        )
        copies[-1].start()
    own = pltpu.make_async_copy(src_ref.at[me], dst_ref.at[me], own_sem)
    own.start()
    return copies + [own]


def kernel(
    nv, pos_ref, alt_ref, gm_ref, gb_ref, gx_ref, gd_ref, rows_ref, base_ref, rate_ref, residue_ref, skip_ref,
    out_ref, effect_ref, score_ref,
    mine_ref, got_ref, back_ref, enter_ref, inner_ref, delta_ref, pad_ref, parts_ref, sums_ref,
    own_sems, send_sems, recv_sems,
):
    length, width = out_ref.shape
    devices, me = lax.axis_size("context"), lax.axis_index("context")
    share = width // devices
    tiles = share // 128
    half, stretch = length // 2, length // nv
    chunk = 512
    chunks, owners = width // chunk, chunk // share
    step = lax.broadcasted_iota(jnp.int32, (stretch, 1), 0)
    pick = lax.broadcasted_iota(jnp.int32, (base_ref.shape[1], 1), 0)
    places = [lax.rem(pos_ref[me * nv + i], stretch) for i in range(nv)]
    alts = [alt_ref[me * nv + i] for i in range(nv)]
    slabs = [slice(i * stretch, (i + 1) * stretch) for i in range(nv)]

    def columns(j):
        return pl.ds(pl.multiple_of(j * chunk, chunk), chunk)

    def force(cols):
        return rows_ref[1, :, cols].astype(F32) * rows_ref[2, :, cols].astype(F32)

    def force_steps(forcing, cols):
        table = base_ref[1, :, cols].astype(F32) * base_ref[2, :, cols].astype(F32)
        steps = []
        for i in range(nv):
            new = jnp.sum(jnp.where(pick == alts[i], table, 0.0), axis=0, keepdims=True)
            steps.append(jnp.where(step == places[i], new - forcing[slabs[i]], 0.0))
        return steps

    barrier_wait = greet(devices)

    def moments(j, carry):
        cols = columns(j)
        forcing = force(cols)
        sums = jnp.dot(gm_ref[...], split3_rhs(forcing), preferred_element_type=F32)
        steps = [jnp.sum(part, axis=0, keepdims=True) for part in force_steps(forcing, cols)]
        packed = jnp.concatenate([sums[:KD]] + steps, axis=0)
        for d in range(owners):
            for c in range(tiles):
                lanes = (d * tiles + c) * 128
                mine_ref[j * owners + d, c * (KD + nv) : (c + 1) * (KD + nv), :] = packed[:, lanes : lanes + 128]
        return carry

    lax.fori_loop(0, chunks, moments, 0)
    barrier_wait()
    first_leg = hand_out(mine_ref, got_ref, own_sems.at[0], send_sems.at[0], recv_sems.at[0])

    def local(j, carry):
        cols = columns(j)
        forcing = force(cols)
        skip = skip_ref[:, cols]
        rate = rate_ref[:, cols]
        terms = cheb_terms(rate, KD)
        coef = modal_coef(rate, residue_ref[:, cols])
        lead = coef * jnp.exp(-rate)
        weights = [jnp.sum(coef * term, axis=0, keepdims=True) for term in terms]
        filtered = []
        for b in range(2):
            products = jnp.dot(
                gb_ref[...], split3_rhs(forcing[b * half : (b + 1) * half]), preferred_element_type=F32
            )
            total = weights[0] * products[:half]
            for k in range(1, KB):
                total = total + weights[k] * products[k * half : (k + 1) * half]
            filtered.append(total)
            if b == 0:
                first = products[KB * half : KB * half + KB]
        state = terms[0] * first[0:1]
        for k in range(1, KB):
            state = state + terms[k] * first[k : k + 1]
        state = lead * state
        zeros = jnp.zeros((16, chunk), F32)
        cross = [jnp.sum(terms[k] * state, axis=0, keepdims=True) for k in range(KB)]
        z = jnp.concatenate(cross + [zeros[: 16 - KB]], axis=0)
        filtered[1] = filtered[1] + jnp.dot(gx_ref[...], split3_rhs(z), preferred_element_type=F32)
        inner_ref[:, cols] = jnp.concatenate(filtered, axis=0) + skip * forcing

        z = jnp.concatenate(weights + [zeros[: 16 - KD]], axis=0)
        impulse = jnp.dot(gd_ref[...], split3_rhs(z), preferred_element_type=F32)
        for c in range(chunk // 128):
            pad_ref[c, length:, :] = impulse[:, c * 128 : (c + 1) * 128]
        steps = force_steps(forcing, cols)
        deltas = [skip * part for part in steps]
        for i in range(nv):
            impact = jnp.sum(steps[i], axis=0, keepdims=True)
            for j2 in range(i, nv):
                response = jnp.concatenate(
                    [
                        pad_ref[c, pl.ds(length + (j2 - i) * stretch - places[i], stretch), :]
                        for c in range(chunk // 128)
                    ],
                    axis=1,
                )
                deltas[j2] = deltas[j2] + response * impact
        for i in range(nv):
            delta_ref[slabs[i], cols] = deltas[i]
        return carry

    for c in range(chunk // 128):
        pad_ref[c, :length, :] = jnp.zeros((length, 128), F32)
    early = chunks // 2
    lax.fori_loop(0, early, local, 0)

    for copy in first_leg:
        copy.wait()
    mine = pl.ds(pl.multiple_of(me * share, share), share)
    row = lax.broadcasted_iota(jnp.int32, (devices, 128), 0)
    lags = []
    for i in range(nv):
        lag = jnp.zeros((devices, 128), F32)
        for d in range(devices):
            gap = (length - 1 + d * length - pos_ref[d * nv + i]).astype(F32)
            lag = jnp.where(row == d, gap, lag)
        lags.append(lag)
    combine(nv, length, lags, got_ref, rate_ref[:, mine], residue_ref[:, mine], back_ref)
    second_leg = hand_out(back_ref, enter_ref, own_sems.at[1], send_sems.at[1], recv_sems.at[1])
    lax.fori_loop(early, chunks, local, 0)
    for copy in second_leg:
        copy.wait()

    def finish(j, carry):
        cols = columns(j)
        q = rows_ref[0, :, cols].astype(F32)
        entering = jnp.concatenate(
            [
                enter_ref[j * owners + d, c * 2 * KD : (c + 1) * 2 * KD, :]
                for d in range(owners)
                for c in range(tiles)
            ],
            axis=1,
        )
        zeros = jnp.zeros((16 - KD, chunk), F32)
        z = jnp.concatenate([entering[:KD], zeros], axis=0)
        inner = inner_ref[:, cols] + jnp.dot(gd_ref[...], split3_rhs(z), preferred_element_type=F32)
        out_ref[:, cols] = (q * inner).astype(out_ref.dtype)
        z = jnp.concatenate([entering[KD:], zeros], axis=0)
        delta = delta_ref[:, cols] + jnp.dot(gd_ref[...], split3_rhs(z), preferred_element_type=F32)
        table = base_ref[0, :, cols].astype(F32)
        total = jnp.zeros((1, chunk), F32)
        for i in range(nv):
            new = jnp.sum(jnp.where(pick == alts[i], table, 0.0), axis=0, keepdims=True)
            gate = q[slabs[i]]
            gate_step = jnp.where(step == places[i], new - gate, 0.0)
            change = (gate + gate_step) * delta[slabs[i]] + gate_step * inner[slabs[i]]
            effect_ref[slabs[i], cols] = change.astype(effect_ref.dtype)
            total = total + jnp.sum(change, axis=0, keepdims=True)
        for d in range(owners):
            for c in range(tiles):
                lanes = (d * tiles + c) * 128
                parts_ref[j * owners + d, c : c + 1, :] = total[:, lanes : lanes + 128]
        return carry

    lax.fori_loop(0, chunks, finish, 0)
    for copy in hand_out(parts_ref, sums_ref, own_sems.at[2], send_sems.at[2], recv_sems.at[2]):
        copy.wait()
    score_ref[...] = jnp.sum(sums_ref[...], axis=0)


def on_device(features, base_rows, positions, alt_bases, decay_rate, residue, skip_gain):
    length, _, width = features.shape
    devices = lax.axis_size("context")
    nv = positions.shape[0] // devices
    share = width // devices
    tiles = share // 128
    half = length // 2
    table = cheb_table(length)

    gm = jnp.asarray(split3_lhs(pad_rows(table[::-1, :KD].T, 16)))
    lag = np.arange(half)[:, None] - np.arange(half)[None]
    toeplitz = np.where((lag >= 0)[None], table[np.maximum(lag, 0), :KB].transpose(2, 0, 1), 0.0)
    toeplitz = toeplitz.reshape(KB * half, half)
    ends = pad_rows(table[:half, :KB][::-1].T, 8)
    gb = jnp.asarray(split3_lhs(np.concatenate([toeplitz, ends], axis=0)))
    gx = jnp.asarray(split3_lhs(pad_cols(table[:half, :KB], 16)))
    gd = jnp.asarray(split3_lhs(pad_cols(table[:, :KD], 16)))

    smem = pl.BlockSpec(memory_space=pltpu.SMEM)
    vmem = pl.BlockSpec(memory_space=pltpu.VMEM)
    ref_out, effect, channel_score = pl.pallas_call(
        functools.partial(kernel, nv),
        in_specs=[smem, smem] + [vmem] * 9,
        out_specs=[vmem] * 3,
        out_shape=[
            jax.ShapeDtypeStruct((length, width), BF16),
            jax.ShapeDtypeStruct((length, width), BF16),
            jax.ShapeDtypeStruct((tiles, 128), F32),
        ],
        scratch_shapes=[
            pltpu.VMEM((devices, tiles * (KD + nv), 128), F32),
            pltpu.VMEM((devices, tiles * (KD + nv), 128), F32),
            pltpu.VMEM((devices, tiles * 2 * KD, 128), F32),
            pltpu.VMEM((devices, tiles * 2 * KD, 128), F32),
            pltpu.VMEM((length, width), F32),
            pltpu.VMEM((length, width), F32),
            pltpu.VMEM((4, 2 * length, 128), F32),
            pltpu.VMEM((devices, tiles, 128), F32),
            pltpu.VMEM((devices, tiles, 128), F32),
            pltpu.SemaphoreType.DMA((3,)),
            pltpu.SemaphoreType.DMA((3, devices)),
            pltpu.SemaphoreType.DMA((3, devices)),
        ],
        compiler_params=pltpu.CompilerParams(collective_id=0, has_side_effects=True),
        name="score_variants",
    )(
        positions, alt_bases, gm, gb, gx, gd, features.transpose(1, 0, 2), base_rows.transpose(1, 0, 2),
        decay_rate, residue, skip_gain.reshape(1, width),
    )
    return ref_out, effect, channel_score.reshape(share)


def solution(mesh):
    return jax.shard_map(
        on_device,
        mesh=mesh,
        in_specs=(P(("group", "context"), None, None), P(), P("group"), P("group"), P(), P(), P()),
        out_specs=(
            P(("group", "context"), None),
            P(("group", "context"), None),
            P(("group", "context")),
        ),
        check_vma=False,
    )
```

profile of v0, /device:TPU:0, one launch (start us, length us, event | category | flops | bytes accessed | tf_op | source)
XLA Modules:
  0.0 56.8 jit_solution(9449485528887503257)
XLA Ops:
  0.6 51.0 %score_variants.1 = (bf16[128,8192]{1,0:T(8,128)(2,1)}, bf16[128,8192]{1,0:T(8,128)(2,1)}, f32[4,128]{1,0:T(4,128)}) custom-call(s32[64]{0:T(128)} %pos_ref.1, s32[64]{0:T(128)} %alt_ref.1, bf16[16,384]{1,0:T(8,128)(2,1)} %constant.8.clone.gm_ref, bf16[456,192]{1,0:T(8,128)(2,1)} %constant.9.clone.gb_ref, bf16[64,48]{1,0:T(8,128)(2,1)} %constant.10.clone.gx_ref, ...), custom_call_target="tpu_custom_call" | custom-call | tf_op jit(solution)/shard_map/score_variants/pallas_call | solution.py:319
  51.7 0.0 copy-start
  51.7 3.2 %copy.17 = bf16[128,8192]{1,0:T(8,128)(2,1)} copy(bf16[128,8192]{1,0:T(8,128)(2,1)} %get-tuple-element.12) | data formatting | bytes 4194304
  54.9 0.0 copy-done
  54.9 0.0 copy-start.1
  54.9 1.3 %copy.18 = bf16[128,8192]{1,0:T(8,128)(2,1)} copy(bf16[128,8192]{1,0:T(8,128)(2,1)S(1)} %copy-done) | data formatting | bytes 4194304
  56.3 0.0 copy-done.1
  56.3 0.6 %copy.19 = f32[512]{0:T(512)} copy(f32[512]{0:T(512)S(1)} %bitcast.7) | data formatting | bytes 4096
Async XLA Ops:
  51.7 3.3 %copy-start = (bf16[128,8192]{1,0:T(8,128)(2,1)S(1)}, bf16[128,8192]{1,0:T(8,128)(2,1)}, u32[]{:S(2)}) copy-start(bf16[128,8192]{1,0:T(8,128)(2,1)} %get-tuple-element.13) | copy-start | bytes 6291460
  54.9 1.3 %copy-start.1 = (f32[4,128]{1,0:T(4,128)S(1)}, f32[4,128]{1,0:T(4,128)}, u32[]{:S(2)}) copy-start(f32[4,128]{1,0:T(4,128)} %get-tuple-element.8) | copy-start | bytes 6148
where the time goes:
time: 57 us; the launch traced here: 56.8 us
  Pallas kernels  51 us (89%)
  local copies, waits for them, and re-layouts  5.15 us (9%)
  between operations  0.65 us (1%)
    pallas_call x1, Pallas kernels, on_device(): pl.pallas_call(functools.partial(kernel, nv), in_specs=[smem, smem] + [vm...  51 us
    unnamed x7, local copies, waits for them, and re-layouts  5.15 us

commit v1 on v0

--- a/solution.py
+++ b/solution.py
@@ -13,6 +13,7 @@
 MESH = pl.DeviceIdType.MESH
 RATE_MAX = 0.03
 KD = 10
+KF = 6
 KB = 7
 
 
@@ -62,9 +63,10 @@
     return residue * jnp.sqrt(z * tail)
 
 
-def combine(nv, length, lags, in_ref, my_rate, my_residue, out_ref):
+def combine(nv, length, lags, in_ref, low_ref, my_rate, my_residue, out_ref, out_low_ref, part):
     devices = in_ref.shape[0]
-    height = KD + nv
+    height = KF + nv
+    small = KD - KF
     row = lax.broadcasted_iota(jnp.int32, (devices, 128), 0)
 
     def before(ends, rate_n):
@@ -76,13 +78,14 @@
             hop *= 2
         return ends
 
-    for c in range(my_rate.shape[1] // 128):
+    for c in part:
         rate = my_rate[:, c * 128 : (c + 1) * 128]
         terms = cheb_terms(rate, KD)
         lead = modal_coef(rate, my_residue[:, c * 128 : (c + 1) * 128]) * jnp.exp(-rate)
         leads = [lead * term for term in terms]
-        moments = [in_ref[:, c * height + k, :] for k in range(KD)]
-        subs = [in_ref[:, c * height + KD + i, :] for i in range(nv)]
+        moments = [in_ref[:, c * height + k, :] for k in range(KF)]
+        moments += [low_ref[:, c * small + k, :] for k in range(small)]
+        subs = [in_ref[:, c * height + KF + i, :] for i in range(nv)]
         base = [jnp.zeros((devices, 128), F32) for _ in range(KD)]
         change = [jnp.zeros((devices, 128), F32) for _ in range(KD)]
         for n in range(rate.shape[0]):
@@ -97,9 +100,12 @@
             for k in range(KD):
                 base[k] = base[k] + leads[k][n : n + 1] * ends
                 change[k] = change[k] + leads[k][n : n + 1] * shifted
-        for k in range(KD):
-            out_ref[:, c * 2 * KD + k, :] = base[k]
-            out_ref[:, c * 2 * KD + KD + k, :] = change[k]
+        for k in range(KF):
+            out_ref[:, c * 2 * KF + k, :] = base[k]
+            out_ref[:, c * 2 * KF + KF + k, :] = change[k]
+        for k in range(small):
+            out_low_ref[:, c * 2 * small + k, :] = base[KF + k]
+            out_low_ref[:, c * 2 * small + small + k, :] = change[KF + k]
 
 
 def greet(devices):
@@ -112,33 +118,35 @@
     return lambda: pl.semaphore_wait(barrier, devices - 1)
 
 
-def hand_out(src_ref, dst_ref, own_sem, send_sems, recv_sems):
+def hand_out(src_ref, dst_ref, send_sems, recv_sems, leg, hops=None, first=0, count=None):
     devices = src_ref.shape[0]
     me = lax.axis_index("context")
+    rows = pl.ds(first, src_ref.shape[1] if count is None else count)
     copies = []
-    for hop in range(1, devices):
-        peer = lax.rem(me + hop, devices)
-        copies.append(
-            pltpu.make_async_remote_copy(
-                src_ref=src_ref.at[peer],
-                dst_ref=dst_ref.at[me],
-                send_sem=send_sems.at[hop],
-                recv_sem=recv_sems.at[hop],
-                device_id={"context": peer},
-                device_id_type=MESH,
+    for hop in range(devices) if hops is None else hops:
+        if hop == 0:
+            copies.append(pltpu.make_async_copy(src_ref.at[me, rows], dst_ref.at[me, rows], send_sems.at[leg, 0]))
+        else:
+            peer = lax.rem(me + hop, devices)
+            copies.append(
+                pltpu.make_async_remote_copy(
+                    src_ref=src_ref.at[peer, rows],
+                    dst_ref=dst_ref.at[me, rows],
+                    send_sem=send_sems.at[leg, hop],
+                    recv_sem=recv_sems.at[leg, hop],
+                    device_id={"context": peer},
+                    device_id_type=MESH,
+                )
             )
-        )
         copies[-1].start()
-    own = pltpu.make_async_copy(src_ref.at[me], dst_ref.at[me], own_sem)
-    own.start()
-    return copies + [own]
+    return copies
 
 
 def kernel(
     nv, pos_ref, alt_ref, gm_ref, gb_ref, gx_ref, gd_ref, rows_ref, base_ref, rate_ref, residue_ref, skip_ref,
     out_ref, effect_ref, score_ref,
-    mine_ref, got_ref, back_ref, enter_ref, inner_ref, delta_ref, pad_ref, parts_ref, sums_ref,
-    own_sems, send_sems, recv_sems,
+    mine_ref, got_ref, back_ref, enter_ref, mine_low_ref, got_low_ref, back_low_ref, enter_low_ref,
+    low_in_ref, low_out_ref, inner_ref, delta_ref, pad_ref, parts_ref, sums_ref, send_sems, recv_sems,
 ):
     length, width = out_ref.shape
     devices, me = lax.axis_size("context"), lax.axis_index("context")
@@ -147,6 +155,7 @@
     half, stretch = length // 2, length // nv
     chunk = 512
     chunks, owners = width // chunk, chunk // share
+    small = KD - KF
     step = lax.broadcasted_iota(jnp.int32, (stretch, 1), 0)
     pick = lax.broadcasted_iota(jnp.int32, (base_ref.shape[1], 1), 0)
     places = [lax.rem(pos_ref[me * nv + i], stretch) for i in range(nv)]
@@ -170,20 +179,30 @@
     barrier_wait = greet(devices)
 
     def moments(j, carry):
+        j = lax.rem(me // owners + j, chunks)
         cols = columns(j)
         forcing = force(cols)
         sums = jnp.dot(gm_ref[...], split3_rhs(forcing), preferred_element_type=F32)
         steps = [jnp.sum(part, axis=0, keepdims=True) for part in force_steps(forcing, cols)]
-        packed = jnp.concatenate([sums[:KD]] + steps, axis=0)
+        packed = jnp.concatenate([sums[:KF]] + steps, axis=0)
         for d in range(owners):
+            low = []
             for c in range(tiles):
                 lanes = (d * tiles + c) * 128
-                mine_ref[j * owners + d, c * (KD + nv) : (c + 1) * (KD + nv), :] = packed[:, lanes : lanes + 128]
+                mine_ref[j * owners + d, c * (KF + nv) : (c + 1) * (KF + nv), :] = packed[:, lanes : lanes + 128]
+                low.append(sums[KF:KD, lanes : lanes + 128])
+            mine_low_ref[j * owners + d] = jnp.concatenate(low, axis=0).astype(BF16)
         return carry
 
-    lax.fori_loop(0, chunks, moments, 0)
+    lax.fori_loop(0, chunks // 2, moments, 0)
     barrier_wait()
-    first_leg = hand_out(mine_ref, got_ref, own_sems.at[0], send_sems.at[0], recv_sems.at[0])
+    near = range(1, devices // 2 - owners + 1)
+    rest = [hop for hop in range(devices) if hop not in near]
+    first_leg = hand_out(mine_ref, got_ref, send_sems, recv_sems, 0, near)
+    first_leg += hand_out(mine_low_ref, got_low_ref, send_sems, recv_sems, 1, near)
+    lax.fori_loop(chunks // 2, chunks, moments, 0)
+    first_leg += hand_out(mine_ref, got_ref, send_sems, recv_sems, 0, rest)
+    first_leg += hand_out(mine_low_ref, got_low_ref, send_sems, recv_sems, 1, rest)
 
     def local(j, carry):
         cols = columns(j)
@@ -252,8 +271,21 @@
             gap = (length - 1 + d * length - pos_ref[d * nv + i]).astype(F32)
             lag = jnp.where(row == d, gap, lag)
         lags.append(lag)
-    combine(nv, length, lags, got_ref, rate_ref[:, mine], residue_ref[:, mine], back_ref)
-    second_leg = hand_out(back_ref, enter_ref, own_sems.at[1], send_sems.at[1], recv_sems.at[1])
+    low_in_ref[...] = got_low_ref[...].astype(F32)
+    pieces = 2 if tiles > 1 else 1
+    span = tiles // pieces
+    second_leg = []
+    for p in range(pieces):
+        combine(
+            nv, length, lags, got_ref, low_in_ref, rate_ref[:, mine], residue_ref[:, mine], back_ref, low_out_ref,
+            range(p * span, (p + 1) * span),
+        )
+        first, count = p * span * 2 * small, span * 2 * small
+        back_low_ref[:, first : first + count, :] = low_out_ref[:, first : first + count, :].astype(BF16)
+        second_leg += hand_out(
+            back_ref, enter_ref, send_sems, recv_sems, 2 + p, None, p * span * 2 * KF, span * 2 * KF
+        )
+        second_leg += hand_out(back_low_ref, enter_low_ref, send_sems, recv_sems, 4 + p, None, first, count)
     lax.fori_loop(early, chunks, local, 0)
     for copy in second_leg:
         copy.wait()
@@ -261,19 +293,18 @@
     def finish(j, carry):
         cols = columns(j)
         q = rows_ref[0, :, cols].astype(F32)
-        entering = jnp.concatenate(
-            [
-                enter_ref[j * owners + d, c * 2 * KD : (c + 1) * 2 * KD, :]
-                for d in range(owners)
-                for c in range(tiles)
-            ],
-            axis=1,
-        )
+        lead, tail = [], []
+        for d in range(owners):
+            low = enter_low_ref[j * owners + d].astype(F32)
+            for c in range(tiles):
+                lead.append(enter_ref[j * owners + d, c * 2 * KF : (c + 1) * 2 * KF, :])
+                tail.append(low[c * 2 * small : (c + 1) * 2 * small])
+        lead, tail = jnp.concatenate(lead, axis=1), jnp.concatenate(tail, axis=1)
         zeros = jnp.zeros((16 - KD, chunk), F32)
-        z = jnp.concatenate([entering[:KD], zeros], axis=0)
+        z = jnp.concatenate([lead[:KF], tail[:small], zeros], axis=0)
         inner = inner_ref[:, cols] + jnp.dot(gd_ref[...], split3_rhs(z), preferred_element_type=F32)
         out_ref[:, cols] = (q * inner).astype(out_ref.dtype)
-        z = jnp.concatenate([entering[KD:], zeros], axis=0)
+        z = jnp.concatenate([lead[KF:], tail[small:], zeros], axis=0)
         delta = delta_ref[:, cols] + jnp.dot(gd_ref[...], split3_rhs(z), preferred_element_type=F32)
         table = base_ref[0, :, cols].astype(F32)
         total = jnp.zeros((1, chunk), F32)
@@ -291,7 +322,7 @@
         return carry
 
     lax.fori_loop(0, chunks, finish, 0)
-    for copy in hand_out(parts_ref, sums_ref, own_sems.at[2], send_sems.at[2], recv_sems.at[2]):
+    for copy in hand_out(parts_ref, sums_ref, send_sems, recv_sems, 6):
         copy.wait()
     score_ref[...] = jnp.sum(sums_ref[...], axis=0)
 
@@ -326,20 +357,27 @@
             jax.ShapeDtypeStruct((tiles, 128), F32),
         ],
         scratch_shapes=[
-            pltpu.VMEM((devices, tiles * (KD + nv), 128), F32),
-            pltpu.VMEM((devices, tiles * (KD + nv), 128), F32),
-            pltpu.VMEM((devices, tiles * 2 * KD, 128), F32),
-            pltpu.VMEM((devices, tiles * 2 * KD, 128), F32),
+            pltpu.VMEM((devices, tiles * (KF + nv), 128), F32),
+            pltpu.VMEM((devices, tiles * (KF + nv), 128), F32),
+            pltpu.VMEM((devices, tiles * 2 * KF, 128), F32),
+            pltpu.VMEM((devices, tiles * 2 * KF, 128), F32),
+            pltpu.VMEM((devices, tiles * (KD - KF), 128), BF16),
+            pltpu.VMEM((devices, tiles * (KD - KF), 128), BF16),
+            pltpu.VMEM((devices, tiles * 2 * (KD - KF), 128), BF16),
+            pltpu.VMEM((devices, tiles * 2 * (KD - KF), 128), BF16),
+            pltpu.VMEM((devices, tiles * (KD - KF), 128), F32),
+            pltpu.VMEM((devices, tiles * 2 * (KD - KF), 128), F32),
             pltpu.VMEM((length, width), F32),
             pltpu.VMEM((length, width), F32),
             pltpu.VMEM((4, 2 * length, 128), F32),
             pltpu.VMEM((devices, tiles, 128), F32),
             pltpu.VMEM((devices, tiles, 128), F32),
-            pltpu.SemaphoreType.DMA((3,)),
-            pltpu.SemaphoreType.DMA((3, devices)),
-            pltpu.SemaphoreType.DMA((3, devices)),
+            pltpu.SemaphoreType.DMA((7, devices)),
+            pltpu.SemaphoreType.DMA((7, devices)),
         ],
-        compiler_params=pltpu.CompilerParams(collective_id=0, has_side_effects=True),
+        compiler_params=pltpu.CompilerParams(
+            collective_id=0, has_side_effects=True, vmem_limit_bytes=36 << 20
+        ),
         name="score_variants",
     )(
         positions, alt_bases, gm, gb, gx, gd, features.transpose(1, 0, 2), base_rows.transpose(1, 0, 2),

time: 57 us -> 57 us (level)
  Pallas kernels: 51 us -> 41.6 us
  local copies, waits for them, and re-layouts: 5.15 us -> 14.2 us
    pallas_call x1, Pallas kernels: 51 us -> 41.6 us  [on_device(): pl.pallas_call(functools.partial(kernel, nv), in_specs=[smem, smem] + [vm...]
    unnamed x7 -> x25, local copies, waits for them, and re-layouts: 5.15 us -> 14.2 us
where the time goes in v1:
time: 57 us; the launch traced here: 56.5 us
  Pallas kernels  41.6 us (73%)
  local copies, waits for them, and re-layouts  14.2 us (25%)
  between operations  0.66 us (1%)
    pallas_call x1, Pallas kernels, on_device(): pl.pallas_call(functools.partial(kernel, nv), in_specs=[smem, smem] + [vm...  41.6 us
    unnamed x25, local copies, waits for them, and re-layouts  14.2 us

profile of v1, /device:TPU:0, one launch (start us, length us, event | category | flops | bytes accessed | tf_op | source)
XLA Modules:
  0.0 56.5 jit_solution(4102446655680679032)
XLA Ops:
  0.6 0.0 copy-start
  0.6 2.8 %copy-done = bf16[128,3,8192]{2,0,1:T(8,128)(2,1)S(1)} copy-done((bf16[128,3,8192]{2,0,1:T(8,128)(2,1)S(1)}, bf16[128,3,8192]{2,0,1:T(8,128)(2,1)}, u32[]{:S(2)}) %copy-start) | copy-done | bytes 6291480
  3.4 0.0 copy-start.1
  3.4 1.0 %copy-done.1 = f32[16,8192]{1,0:T(8,128)S(1)} copy-done((f32[16,8192]{1,0:T(8,128)S(1)}, f32[16,8192]{1,0:T(8,128)}, u32[]{:S(2)}) %copy-start.1) | copy-done | bytes 524312
  4.5 1.0 %copy-done.2 = f32[16,8192]{1,0:T(8,128)S(1)} copy-done((f32[16,8192]{1,0:T(8,128)S(1)}, f32[16,8192]{1,0:T(8,128)}, u32[]{:S(2)}) %copy-start.2) | copy-done | bytes 524312
  5.5 0.0 copy-start.3
  5.5 0.9 %copy-done.3 = bf16[456,192]{1,0:T(8,128)(2,1)S(1)} copy-done((bf16[456,192]{1,0:T(8,128)(2,1)S(1)}, bf16[456,192]{1,0:T(8,128)(2,1)}, u32[]{:S(2)}) %copy-start.3) | copy-done | bytes 175128
  6.4 0.0 copy-start.4
  6.4 0.9 %copy-done.4 = bf16[4,3,8192]{2,0,1:T(4,128)(2,1)S(1)} copy-done((bf16[4,3,8192]{2,0,1:T(4,128)(2,1)S(1)}, bf16[4,3,8192]{2,0,1:T(4,128)(2,1)}, u32[]{:S(2)}) %copy-start.4) | copy-done | bytes 196632
  7.4 0.8 %copy-done.5 = f32[8192]{0:T(1024)S(1)} copy-done((f32[8192]{0:T(1024)S(1)}, f32[8192]{0:T(1024)}, u32[]{:S(2)}) %copy-start.5) | copy-done | bytes 32792
  8.1 0.0 copy-start.6
  8.1 0.8 %copy-done.6 = bf16[128,48]{1,0:T(8,128)(2,1)S(1)} copy-done((bf16[128,48]{1,0:T(8,128)(2,1)S(1)}, bf16[128,48]{1,0:T(8,128)(2,1)}, u32[]{:S(2)}) %copy-start.6) | copy-done | bytes 12312
  8.9 0.0 copy-start.7
  8.9 0.7 %copy-done.7 = bf16[64,48]{1,0:T(8,128)(2,1)S(1)} copy-done((bf16[64,48]{1,0:T(8,128)(2,1)S(1)}, bf16[64,48]{1,0:T(8,128)(2,1)}, u32[]{:S(2)}) %copy-start.7) | copy-done | bytes 6168
  9.6 0.0 copy-start.8
  9.6 0.7 %copy-done.8 = bf16[16,384]{1,0:T(8,128)(2,1)S(1)} copy-done((bf16[16,384]{1,0:T(8,128)(2,1)S(1)}, bf16[16,384]{1,0:T(8,128)(2,1)}, u32[]{:S(2)}) %copy-start.8) | copy-done | bytes 12312
  10.3 0.0 copy-start.9
  10.3 0.7 %copy-done.9 = s32[64]{0:T(128)S(1)} copy-done((s32[64]{0:T(128)S(1)}, s32[64]{0:T(128)}, u32[]{:S(2)}) %copy-start.9) | copy-done | bytes 280
  11.0 0.0 copy-start.10
  11.0 0.7 %copy-done.10 = s32[64]{0:T(128)S(1)} copy-done((s32[64]{0:T(128)S(1)}, s32[64]{0:T(128)}, u32[]{:S(2)}) %copy-start.10) | copy-done | bytes 280
  11.6 41.6 %score_variants.1 = (bf16[128,8192]{1,0:T(8,128)(2,1)S(1)}, bf16[128,8192]{1,0:T(8,128)(2,1)S(1)}, f32[4,128]{1,0:T(4,128)S(1)}) custom-call(s32[64]{0:T(128)S(1)} %copy-done.9, s32[64]{0:T(128)S(1)} %copy-done.10, bf16[16,384]{1,0:T(8,128)(2,1)S(1)} %copy-done.8, bf16[456,192]{1,0:T(8,128)(2,1)S(1)} %copy-done.3, bf16[64,48]{1,0:T(8,128)(2,1)S(1)} %copy-done.7, ...), custom_call_target="tpu_custom_call" | custom-call | tf_op jit(solution)/shard_map/score_variants/pallas_call | solution.py:350
  53.2 1.3 %copy.17 = bf16[128,8192]{1,0:T(8,128)(2,1)} copy(bf16[128,8192]{1,0:T(8,128)(2,1)S(1)} %get-tuple-element.12) | data formatting | bytes 4194304
  54.6 1.3 %copy.18 = bf16[128,8192]{1,0:T(8,128)(2,1)} copy(bf16[128,8192]{1,0:T(8,128)(2,1)S(1)} %get-tuple-element.13) | data formatting | bytes 4194304
  55.9 0.6 %copy.19 = f32[512]{0:T(512)} copy(f32[512]{0:T(512)S(1)} %bitcast.7) | data formatting | bytes 4096
  (2 shorter events, 0.0 us)
Async XLA Ops:
  0.6 2.8 %copy-start = (bf16[128,3,8192]{2,0,1:T(8,128)(2,1)S(1)}, bf16[128,3,8192]{2,0,1:T(8,128)(2,1)}, u32[]{:S(2)}) copy-start(bf16[128,3,8192]{2,0,1:T(8,128)(2,1)} %param.11) | copy-start | bytes 18874372
  3.4 1.0 %copy-start.1 = (f32[16,8192]{1,0:T(8,128)S(1)}, f32[16,8192]{1,0:T(8,128)}, u32[]{:S(2)}) copy-start(f32[16,8192]{1,0:T(8,128)} %rate_ref.1) | copy-start | bytes 1572868
  4.5 1.0 %copy-start.2 = (f32[16,8192]{1,0:T(8,128)S(1)}, f32[16,8192]{1,0:T(8,128)}, u32[]{:S(2)}) copy-start(f32[16,8192]{1,0:T(8,128)} %residue_ref.1) | copy-start | bytes 1572868
  5.5 0.9 %copy-start.3 = (bf16[456,192]{1,0:T(8,128)(2,1)S(1)}, bf16[456,192]{1,0:T(8,128)(2,1)}, u32[]{:S(2)}) copy-start(bf16[456,192]{1,0:T(8,128)(2,1)} %constant.9.clone.gb_ref) | copy-start | bytes 525316
  6.4 0.9 %copy-start.4 = (bf16[4,3,8192]{2,0,1:T(4,128)(2,1)S(1)}, bf16[4,3,8192]{2,0,1:T(4,128)(2,1)}, u32[]{:S(2)}) copy-start(bf16[4,3,8192]{2,0,1:T(4,128)(2,1)} %param.12) | copy-start | bytes 589828
  7.4 0.8 %copy-start.5 = (f32[8192]{0:T(1024)S(1)}, f32[8192]{0:T(1024)}, u32[]{:S(2)}) copy-start(f32[8192]{0:T(1024)} %param.17) | copy-start | bytes 98308
  8.1 0.8 %copy-start.6 = (bf16[128,48]{1,0:T(8,128)(2,1)S(1)}, bf16[128,48]{1,0:T(8,128)(2,1)}, u32[]{:S(2)}) copy-start(bf16[128,48]{1,0:T(8,128)(2,1)} %constant.11.clone.gd_ref) | copy-start | bytes 36868
  8.9 0.7 %copy-start.7 = (bf16[64,48]{1,0:T(8,128)(2,1)S(1)}, bf16[64,48]{1,0:T(8,128)(2,1)}, u32[]{:S(2)}) copy-start(bf16[64,48]{1,0:T(8,128)(2,1)} %constant.10.clone.gx_ref) | copy-start | bytes 18436
  9.6 0.7 %copy-start.8 = (bf16[16,384]{1,0:T(8,128)(2,1)S(1)}, bf16[16,384]{1,0:T(8,128)(2,1)}, u32[]{:S(2)}) copy-start(bf16[16,384]{1,0:T(8,128)(2,1)} %constant.8.clone.gm_ref) | copy-start | bytes 36868
  10.3 0.7 %copy-start.9 = (s32[64]{0:T(128)S(1)}, s32[64]{0:T(128)}, u32[]{:S(2)}) copy-start(s32[64]{0:T(128)} %pos_ref.1) | copy-start | bytes 772
  11.0 0.7 %copy-start.10 = (s32[64]{0:T(128)S(1)}, s32[64]{0:T(128)}, u32[]{:S(2)}) copy-start(s32[64]{0:T(128)} %alt_ref.1) | copy-start | bytes 772

commit v2 on v1

--- a/solution.py
+++ b/solution.py
@@ -143,8 +143,9 @@
 
 
 def kernel(
-    nv, pos_ref, alt_ref, gm_ref, gb_ref, gx_ref, gd_ref, rows_ref, base_ref, rate_ref, residue_ref, skip_ref,
-    out_ref, effect_ref, score_ref,
+    nv, pos_in, alt_in, gm_in, gb_in, gx_in, gd_in, rows_in, base_in, rate_in, residue_in, skip_in,
+    out_hbm, effect_hbm, score_ref,
+    out_ref, effect_ref, pos_ref, alt_ref, gm_ref, gb_ref, gx_ref, gd_ref, rows_ref, base_ref, rate_ref, residue_ref, skip_ref, load_sems,
     mine_ref, got_ref, back_ref, enter_ref, mine_low_ref, got_low_ref, back_low_ref, enter_low_ref,
     low_in_ref, low_out_ref, inner_ref, delta_ref, pad_ref, parts_ref, sums_ref, send_sems, recv_sems,
 ):
@@ -156,6 +157,18 @@
     chunk = 512
     chunks, owners = width // chunk, chunk // share
     small = KD - KF
+    loads = [
+        (pos_in, pos_ref), (alt_in, alt_ref), (base_in, base_ref), (gm_in, gm_ref),
+        (rows_in.at[1], rows_ref.at[1]), (rows_in.at[2], rows_ref.at[2]), (gb_in, gb_ref), (gx_in, gx_ref),
+        (gd_in, gd_ref), (rate_in, rate_ref), (residue_in, residue_ref), (skip_in, skip_ref),
+        (rows_in.at[0], rows_ref.at[0]),
+    ]
+    loads = [pltpu.make_async_copy(src, dst, load_sems.at[i]) for i, (src, dst) in enumerate(loads)]
+    for load in loads:
+        load.start()
+    barrier_wait = greet(devices)
+    for load in loads[:6]:
+        load.wait()
     step = lax.broadcasted_iota(jnp.int32, (stretch, 1), 0)
     pick = lax.broadcasted_iota(jnp.int32, (base_ref.shape[1], 1), 0)
     places = [lax.rem(pos_ref[me * nv + i], stretch) for i in range(nv)]
@@ -175,8 +188,6 @@
             new = jnp.sum(jnp.where(pick == alts[i], table, 0.0), axis=0, keepdims=True)
             steps.append(jnp.where(step == places[i], new - forcing[slabs[i]], 0.0))
         return steps
-
-    barrier_wait = greet(devices)
 
     def moments(j, carry):
         j = lax.rem(me // owners + j, chunks)
@@ -258,6 +269,8 @@
     for c in range(chunk // 128):
         pad_ref[c, :length, :] = jnp.zeros((length, 128), F32)
     early = chunks // 2
+    for load in loads[6:]:
+        load.wait()
     lax.fori_loop(0, early, local, 0)
 
     for copy in first_leg:
@@ -322,9 +335,17 @@
         return carry
 
     lax.fori_loop(0, chunks, finish, 0)
+    stores = [
+        pltpu.make_async_copy(out_ref, out_hbm, load_sems.at[0]),
+        pltpu.make_async_copy(effect_ref, effect_hbm, load_sems.at[1]),
+    ]
+    for store in stores:
+        store.start()
     for copy in hand_out(parts_ref, sums_ref, send_sems, recv_sems, 6):
         copy.wait()
     score_ref[...] = jnp.sum(sums_ref[...], axis=0)
+    for store in stores:
+        store.wait()
 
 
 def on_device(features, base_rows, positions, alt_bases, decay_rate, residue, skip_gain):
@@ -345,18 +366,25 @@
     gx = jnp.asarray(split3_lhs(pad_cols(table[:half, :KB], 16)))
     gd = jnp.asarray(split3_lhs(pad_cols(table[:, :KD], 16)))
 
-    smem = pl.BlockSpec(memory_space=pltpu.SMEM)
+    operands = (
+        positions, alt_bases, gm, gb, gx, gd, features.transpose(1, 0, 2), base_rows.transpose(1, 0, 2),
+        decay_rate, residue, skip_gain.reshape(1, width),
+    )
     vmem = pl.BlockSpec(memory_space=pltpu.VMEM)
     ref_out, effect, channel_score = pl.pallas_call(
         functools.partial(kernel, nv),
-        in_specs=[smem, smem] + [vmem] * 9,
-        out_specs=[vmem] * 3,
+        in_specs=[pl.BlockSpec(memory_space=pltpu.HBM)] * 11,
+        out_specs=[pl.BlockSpec(memory_space=pltpu.HBM)] * 2 + [vmem],
         out_shape=[
             jax.ShapeDtypeStruct((length, width), BF16),
             jax.ShapeDtypeStruct((length, width), BF16),
             jax.ShapeDtypeStruct((tiles, 128), F32),
         ],
-        scratch_shapes=[
+        scratch_shapes=[pltpu.VMEM((length, width), BF16) for _ in range(2)]
+        + [pltpu.SMEM(a.shape, a.dtype) for a in operands[:2]]
+        + [pltpu.VMEM(a.shape, a.dtype) for a in operands[2:]]
+        + [
+            pltpu.SemaphoreType.DMA((13,)),
             pltpu.VMEM((devices, tiles * (KF + nv), 128), F32),
             pltpu.VMEM((devices, tiles * (KF + nv), 128), F32),
             pltpu.VMEM((devices, tiles * 2 * KF, 128), F32),
@@ -376,13 +404,10 @@
             pltpu.SemaphoreType.DMA((7, devices)),
         ],
         compiler_params=pltpu.CompilerParams(
-            collective_id=0, has_side_effects=True, vmem_limit_bytes=36 << 20
+            collective_id=0, has_side_effects=True
         ),
         name="score_variants",
-    )(
-        positions, alt_bases, gm, gb, gx, gd, features.transpose(1, 0, 2), base_rows.transpose(1, 0, 2),
-        decay_rate, residue, skip_gain.reshape(1, width),
-    )
+    )(*operands)
     return ref_out, effect, channel_score.reshape(share)
 
 

time: 57 us -> 49.7 us (0.87)
  local copies, waits for them, and re-layouts: 14.2 us -> 5.15 us
  Pallas kernels: 41.6 us -> 43.8 us
    unnamed x25 -> x7, local copies, waits for them, and re-layouts: 14.2 us -> 5.15 us
    pallas_call x1, Pallas kernels: 41.6 us -> 43.8 us  [on_device(): pl.pallas_call(functools.partial(kernel, nv), in_specs=[pl.BlockSpec(memo...]
where the time goes in v2:
time: 49.7 us; the launch traced here: 49.6 us
  Pallas kernels  43.8 us (88%)
  local copies, waits for them, and re-layouts  5.15 us (10%)
  between operations  0.65 us (1%)
    pallas_call x1, Pallas kernels, on_device(): pl.pallas_call(functools.partial(kernel, nv), in_specs=[pl.BlockSpec(memo...  43.8 us
    unnamed x7, local copies, waits for them, and re-layouts  5.15 us

profile of v2, /device:TPU:0, one launch (start us, length us, event | category | flops | bytes accessed | tf_op | source)
XLA Modules:
  0.0 49.6 jit_solution(8778583192250234848)
XLA Ops:
  0.6 43.8 %score_variants.1 = (bf16[128,8192]{1,0:T(8,128)(2,1)}, bf16[128,8192]{1,0:T(8,128)(2,1)}, f32[4,128]{1,0:T(4,128)}) custom-call(s32[64]{0:T(128)} %pos_in.1, s32[64]{0:T(128)} %alt_in.1, bf16[16,384]{1,0:T(8,128)(2,1)} %constant.8.clone.gm_in, bf16[456,192]{1,0:T(8,128)(2,1)} %constant.9.clone.gb_in, bf16[64,48]{1,0:T(8,128)(2,1)} %constant.10.clone.gx_in, ...), custom_call_target="tpu_custom_call" | custom-call | tf_op jit(solution)/shard_map/score_variants/pallas_call | solution.py:374
  44.4 0.0 copy-start
  44.4 3.2 %copy.17 = bf16[128,8192]{1,0:T(8,128)(2,1)} copy(bf16[128,8192]{1,0:T(8,128)(2,1)} %get-tuple-element.12) | data formatting | bytes 4194304
  47.7 0.0 copy-done
  47.7 0.0 copy-start.1
  47.7 1.3 %copy.18 = bf16[128,8192]{1,0:T(8,128)(2,1)} copy(bf16[128,8192]{1,0:T(8,128)(2,1)S(1)} %copy-done) | data formatting | bytes 4194304
  49.0 0.0 copy-done.1
  49.0 0.6 %copy.19 = f32[512]{0:T(512)} copy(f32[512]{0:T(512)S(1)} %bitcast.7) | data formatting | bytes 4096
Async XLA Ops:
  44.4 3.3 %copy-start = (bf16[128,8192]{1,0:T(8,128)(2,1)S(1)}, bf16[128,8192]{1,0:T(8,128)(2,1)}, u32[]{:S(2)}) copy-start(bf16[128,8192]{1,0:T(8,128)(2,1)} %get-tuple-element.13) | copy-start | bytes 6291460
  47.7 1.3 %copy-start.1 = (f32[4,128]{1,0:T(4,128)S(1)}, f32[4,128]{1,0:T(4,128)}, u32[]{:S(2)}) copy-start(f32[4,128]{1,0:T(4,128)} %get-tuple-element.8) | copy-start | bytes 6148
